TPU v7x, 128 devices: a whole 4x4x4 slice. The times are simulated.
128 devices in a mesh: layer: 2 (over core), latent: 64 (over y, x, z).
Axes of the slice: x: 4, y: 4, z: 4, core: 2. Of those that a mesh axis runs over, the one named last changes fastest.
Arguments:
- activations: bfloat16 [2, 512, 2048], P('layer', 'latent'), may hold values from -15 to 15
- enc_weight: bfloat16 [2, 2048, 65536], P('layer', None, 'latent'), may hold values from -0.09375 to 0.09375
- enc_bias: float32 [65536], P('latent'), may hold values from -3 to 3
- dec_weight: bfloat16 [2, 65536, 2048], P('layer', 'latent'), may hold values from -0.08984375 to 0.08984375
- dec_bias: float32 [2, 2048], P('layer'), may hold values from -3 to 3
- active_mask: int32 [512, 65536], P(None, 'latent'), may hold values 0 or 1
Outputs:
- grad_enc: bfloat16 [2, 2048, 65536], P('layer', None, 'latent')
- grad_dec: bfloat16 [2, 65536, 2048], P('layer', 'latent')
- loss_value: float32 [], replicated
All inputs are finite; a program needn't handle non-finite values. No bound on the sum of `active_mask` on one device may be relied on, other than what follows from the above.
Results may differ from a plain program's by a relative error of at most 0.0065.
Values may be sent and summed in bfloat16 or wider, within the bound.
No kernel may reach another device: no remote copies, remote signals or barrier semaphores. Data moves between devices by JAX's collectives and lax.ppermute only.
A program may use at most 128 MiB of HBM per device.

v0:
```python
import jax
import jax.numpy as jnp
from jax import lax
from jax.sharding import Mesh
from jax.sharding import PartitionSpec as P

LATENT = ("latent_0", "latent_1", "latent_2")
LAYER_LATENT = ("layer", "latent_0", "latent_1", "latent_2")
sparsity_weight = 0.4


def sent_to_all(x, axis):
    count = lax.axis_size(axis)
    return lax.all_to_all(jnp.broadcast_to(x[None], (count, *x.shape)), axis, 0, 0, tiled=True)


def joined_along(blocks, dim):
    blocks = jnp.moveaxis(blocks, 0, dim)
    shape = blocks.shape
    return blocks.reshape(*shape[:dim], shape[dim] * shape[dim + 1], *shape[dim + 2 :])


def collect(x, axis, dim):
    blocks = sent_to_all(x, axis)
    return joined_along(blocks, dim)


def over_axes(x, axes):
    for axis in axes:
        x = lax.psum(x, axis)
    return x


def per_device(activations, enc_weight, enc_bias, dec_weight, dec_bias, active_mask):
    local_rows = activations[0]
    encoder = enc_weight[0]
    decoder = dec_weight[0]
    token_all = collect(local_rows, LATENT, 0)
    layer_pre = jnp.dot(token_all, encoder, preferred_element_type=jnp.float32)
    dec_float = decoder.astype(jnp.float32)
    row_norm = jnp.sqrt(jnp.sum(dec_float * dec_float, axis=1) + 1e-06)
    preact, norm_sum = lax.psum((layer_pre, row_norm), "layer")
    preact = preact + enc_bias
    gating = active_mask.astype(jnp.float32)
    latent_code = preact * gating
    code_b = latent_code.astype(jnp.bfloat16)
    layer_index = lax.axis_index("layer")
    latent_index = lax.axis_index(LATENT)
    partial_value = jnp.dot(code_b, decoder, preferred_element_type=jnp.float32)
    recon = lax.psum(partial_value, LATENT) + dec_bias[0]
    error_full = recon - token_all.astype(jnp.float32)
    error_b = error_full.astype(jnp.bfloat16)
    square_part = jnp.where(latent_index == 0, 0.5 * jnp.sum(error_full * error_full), 0.0)
    layer_grad = jnp.einsum("td,fd->tf", error_b, decoder, preferred_element_type=jnp.float32)
    code_grad = lax.psum(layer_grad, "layer") + sparsity_weight * norm_sum
    preact_grad = (code_grad * gating).astype(jnp.bfloat16)
    grad_enc = jnp.einsum(
        "td,tf->df", token_all, preact_grad, preferred_element_type=jnp.float32
    ).astype(jnp.bfloat16)
    code_total = jnp.sum(latent_code, axis=0)
    shrink = sparsity_weight * code_total[:, None] * dec_float / row_norm[:, None]
    grad_dec = (
        jnp.einsum("tf,td->fd", code_b, error_b, preferred_element_type=jnp.float32) + shrink
    ).astype(jnp.bfloat16)
    sparse_part = jnp.where(
        layer_index == 0, sparsity_weight * jnp.sum(latent_code * norm_sum), 0.0
    )
    loss_total = over_axes(square_part + sparse_part, LAYER_LATENT)
    loss_value = loss_total / (active_mask.shape[0] * token_all.shape[1])
    return (grad_enc[None], grad_dec[None], loss_value)


def solution(mesh):
    torus = Mesh(
        mesh.devices.reshape(mesh.shape["layer"], 4, 4, 4),
        ("layer", "latent_0", "latent_1", "latent_2"),
    )
    placed = (
        P("layer", LATENT, None),
        P("layer", None, LATENT),
        P(LATENT),
        P("layer", LATENT, None),
        P("layer", None),
        P(None, LATENT),
    )
    return jax.shard_map(
        per_device,
        mesh=torus,
        in_specs=placed,
        out_specs=(P("layer", None, LATENT), P("layer", LATENT, None), P()),
        check_vma=False,
    )
```

profile of v0, /device:TPU:0, one launch (start us, length us, event | category | flops | bytes accessed | tf_op | source)
XLA Modules:
  0.0 295.7 jit_solution(14618392666978174406)
XLA Ops:
  7.2 0.0 all-reduce.4.cloned.1.call-start
  7.2 1.0 broadcast_in_dim.9
  8.2 0.0 copy-start.5
  8.2 41.2 %all_to_all.5 = bf16[64,8,2048]{2,1,0:T(8,128)(2,1)S(1)} all-to-all(bf16[64,8,2048]{2,1,0:T(8,128)(2,1)S(1)} %broadcast_in_dim.9), channel_id=1, replica_groups=mesh['layer'=2,'latent_0'=4,'latent_1'=4,'latent_2'=4] {'latent_0','late..., dimensions={0} | all-to-all | bytes 4194304 | tf_op jit(solution)/shard_map/all_to_all | solution.py:14
  49.4 0.0 copy-done.5
  49.4 3.7 %fusion.8 = f32[512,1024]{1,0:T(8,128)} fusion(bf16[1,2048,1024]{2,1,0:T(8,128)(2,1)S(1)} %copy-done.5, bf16[64,8,2048]{2,1,0:T(8,128)(2,1)S(1)} %all_to_all.5), kind=kOutput, calls=%fused_computation.10 | convolution fusion | flops 2147483648 | bytes 8388608 | tf_op jit(solution)/shard_map/dot_general | solution.py:39
  53.1 0.0 all-reduce.4.cloned.1.call-update
  53.1 0.0 copy-start.4
  53.1 0.0 all-reduce.6.cloned.1.call-start
  53.2 3.1 %fusion = f32[1024]{0:T(1024)S(1)} fusion(bf16[1,1024,2048]{2,1,0:T(8,128)(2,1)} %param.9), kind=kLoop, calls=%fused_computation.2 | loop fusion | flops 6290432 | bytes 4198400 | tf_op jit(solution)/shard_map/reduce_sum | solution.py:41
  56.3 2.5 psum.59
  58.8 17.8 %all-reduce.4.cloned.1.call-done = f32[512,1024]{1,0:T(8,128)} async-done(((f32[512,1024]{1,0:T(8,128)}), f32[512,1024]{1,0:T(8,128)}) %all-reduce.4.cloned.1.call-update) | async-done | bytes 2097168 | tf_op jit(solution)/shard_map/psum | solution.py:42
  76.5 0.0 copy-done.4
  76.5 3.6 %multiply_reduce_fusion.1 = (f32[]{:T(128)}, f32[1024]{0:T(1024)S(1)}, bf16[512,1024]{1,0:T(8,128)(2,1)S(1)}) fusion(f32[1024]{0:T(1024)S(1)} %psum.59, s32[512,1024]{1,0:T(8,128)} %param.11, f32[512,1024]{1,0:T(8,128)} %all-reduce.4.cloned.1.call-done, f32[1024]{0:T(1024)S(1)} %copy-done.4), kind=kLoop, calls=%fused_computation.19 | loop fusion | flops 3668991 | bytes 5255172 | tf_op jit(solution)/shard_map/reduce_sum | solution.py:66
  80.1 0.0 copy-done
  80.1 4.4 %fusion.6 = f32[512,2048]{1,0:T(8,128)} fusion(bf16[1,1024,2048]{2,1,0:T(8,128)(2,1)S(1)} %copy-done, bf16[512,1024]{1,0:T(8,128)(2,1)S(1)} %get-tuple-element.8), kind=kOutput, calls=%fused_computation.8 | convolution fusion | flops 2147483648 | bytes 9437184 | tf_op jit(solution)/shard_map/dot_general | solution.py:49
  84.5 0.0 all-reduce.6.cloned.1.call-update
  84.5 0.0 all-reduce.8.cloned.1.call-start
  84.6 140.1 %all-reduce.6.cloned.1.call-done = f32[512,2048]{1,0:T(8,128)} async-done(((f32[512,2048]{1,0:T(8,128)}), f32[512,2048]{1,0:T(8,128)}) %all-reduce.6.cloned.1.call-update) | async-done | bytes 4194320 | tf_op jit(solution)/shard_map/psum | solution.py:50
  224.7 0.0 copy-done.3
  224.7 4.0 %multiply_reduce_fusion = (f32[]{:T(128)}, bf16[512,2048]{1,0:T(8,128)(2,1)S(1)}) fusion(f32[512,2048]{1,0:T(8,128)} %all-reduce.6.cloned.1.call-done, bf16[64,8,2048]{2,1,0:T(8,128)(2,1)S(1)} %all_to_all.5, f32[2048]{0:T(1024)S(1)} %bitcast.32), kind=kLoop, calls=%fused_computation.12 | loop fusion | flops 6291455 | bytes 8396804 | tf_op jit(solution)/shard_map/reduce_sum | solution.py:53
  228.8 1.3 copy-done.2
  230.1 0.0 copy-done.1
  230.1 3.7 %fusion.4 = f32[512,1024]{1,0:T(8,128)} fusion(bf16[512,2048]{1,0:T(8,128)(2,1)S(1)} %get-tuple-element.10, bf16[1,1024,2048]{2,1,0:T(8,128)(2,1)S(1)} %copy-done.1), kind=kOutput, calls=%fused_computation.6 | convolution fusion | flops 2147483648 | bytes 8388608 | tf_op jit(solution)/shard_map/td,fd->tf/dot_general | solution.py:54
  233.8 0.0 all-reduce.8.cloned.1.call-update
  235.1 3.0 %psum.60 = f32[]{:T(128)} all-reduce(f32[]{:T(128)S(6)} %add.76), channel_id=1, replica_groups=mesh['layer'=2,'latent_0'=4,'latent_1'=4,'latent_2'=4] {'layer'}, use_global_device_ids=true, to_apply=%region_8.9 | all-reduce | flops 1 | bytes 8 | tf_op jit(solution)/shard_map/psum | solution.py:30
  238.1 9.3 %psum.61 = f32[]{:T(128)} all-reduce(f32[]{:T(128)} %psum.60), channel_id=1, replica_groups=mesh['layer'=2,'latent_0'=4,'latent_1'=4,'latent_2'=4] {'latent_0'}, use_global_device_ids=true, to_apply=%region_9.10 | all-reduce | flops 1 | bytes 8 | tf_op jit(solution)/shard_map/psum | solution.py:30
  247.4 10.7 %psum.62 = f32[]{:T(128)} all-reduce(f32[]{:T(128)} %psum.61), channel_id=1, replica_groups=mesh['layer'=2,'latent_0'=4,'latent_1'=4,'latent_2'=4] {'latent_1'}, use_global_device_ids=true, to_apply=%region_10.11 | all-reduce | flops 1 | bytes 8 | tf_op jit(solution)/shard_map/psum | solution.py:30
  258.1 9.6 %psum.63 = f32[]{:T(128)} all-reduce(f32[]{:T(128)} %psum.62), channel_id=1, replica_groups=mesh['layer'=2,'latent_0'=4,'latent_1'=4,'latent_2'=4] {'latent_2'}, use_global_device_ids=true, to_apply=%region_11.12 | all-reduce | flops 1 | bytes 8 | tf_op jit(solution)/shard_map/psum | solution.py:30
  268.3 6.7 %fusion.10 = bf16[1,1024,2048]{2,1,0:T(8,128)(2,1)} fusion(f32[1024]{0:T(1024)S(1)} %add_sqrt_fusion, bf16[1,1024,2048]{2,1,0:T(8,128)(2,1)} %param.9, f32[1024]{0:T(1024)S(1)} %broadcast_multiply_fusion, bf16[512,2048]{1,0:T(8,128)(2,1)} %copy-done.2, bf16[512,1024]{1,0:T(8,128)(2,1)S(1)} %get-tuple-element.8), kind=kOutput, calls=%fused_computation.15 | convolution fusion | flops 2157969408 | bytes 11542528 | tf_op jit(solution)/shard_map/tf,td->fd/dot_general | solution.py:63
  275.0 6.7 %convert_bitcast_fusion = bf16[1,2048,1024]{1,2,0:T(8,128)(2,1)} fusion(bf16[64,8,2048]{2,1,0:T(8,128)(2,1)S(1)} %all_to_all.5, f32[512,1024]{1,0:T(8,128)} %all-reduce.8.cloned.1.call-done, s32[512,1024]{1,0:T(8,128)} %param.11, f32[1024]{0:T(1024)S(1)} %broadcast_multiply_fusion.1), kind=kOutput, calls=%fused_computation.13 | convolution fusion | flops 2151677952 | bytes 10489856 | tf_op jit(solution)/shard_map/td,tf->df/dot_general | solution.py:57
  281.7 6.4 %copy.9 = bf16[1,2048,1024]{2,1,0:T(8,128)(2,1)} copy(bf16[1,2048,1024]{1,2,0:T(8,128)(2,1)} %convert_bitcast_fusion) | data formatting | bytes 8388608
  (8 shorter events, 0.0 us)
Async XLA Ops:
  7.2 69.4 %all-reduce.4.cloned.1.call-start = ((), (), s32[]{:S(2)}) async-start(), calls=%async_computation.1 | async-start | bytes 4194304 | tf_op jit(solution)/shard_map/psum | solution.py:42
  8.2 41.2 %copy-start.5 = (bf16[1,2048,1024]{2,1,0:T(8,128)(2,1)S(1)}, bf16[1,2048,1024]{2,1,0:T(8,128)(2,1)}, u32[]{:S(2)}) copy-start(bf16[1,2048,1024]{2,1,0:T(8,128)(2,1)} %param.7) | copy-start | bytes 12582916
  53.1 23.4 %copy-start.4 = (f32[1024]{0:T(1024)S(1)}, f32[1024]{0:T(1024)}, u32[]{:S(2)}) copy-start(f32[1024]{0:T(1024)} %param.8) | copy-start | bytes 12292
  53.1 171.6 %all-reduce.6.cloned.1.call-start = ((), (), s32[]{:S(2)}) async-start(), calls=%async_computation.2 | async-start | bytes 8388608 | tf_op jit(solution)/shard_map/psum | solution.py:50
  76.5 3.6 %copy-start = (bf16[1,1024,2048]{2,1,0:T(8,128)(2,1)S(1)}, bf16[1,1024,2048]{2,1,0:T(8,128)(2,1)}, u32[]{:S(2)}) copy-start(bf16[1,1024,2048]{2,1,0:T(8,128)(2,1)} %param.9) | copy-start | bytes 12582916
  84.5 140.2 %copy-start.3 = (f32[1,2048]{1,0:T(1,128)S(1)}, f32[1,2048]{1,0:T(1,128)}, u32[]{:S(2)}) copy-start(f32[1,2048]{1,0:T(1,128)} %param.10) | copy-start | bytes 24580
  84.5 190.4 %all-reduce.8.cloned.1.call-start = ((), (), s32[]{:S(2)}) async-start(), calls=%async_computation.3 | async-start | bytes 4194304 | tf_op jit(solution)/shard_map/psum | solution.py:55
  224.7 5.4 %copy-start.1 = (bf16[1,1024,2048]{2,1,0:T(8,128)(2,1)S(1)}, bf16[1,1024,2048]{2,1,0:T(8,128)(2,1)}, u32[]{:S(2)}) copy-start(bf16[1,1024,2048]{2,1,0:T(8,128)(2,1)} %param.9) | copy-start | bytes 12582916
  228.8 1.4 copy-start.2
Sparse Core Ops, SparseCore 0:
  53.3 23.2 all-reduce.3
  84.7 140.0 all-reduce.5
  234.0 24.1 all-reduce.7
where the time goes:
time: 296 us
  waiting for transfers between devices  158 us (53%)
  blocking collectives  76.2 us (26%)
  matrix products  25.1 us (8%)
  between operations  16.9 us (6%)
  other arithmetic  10.7 us (4%)
  local copies, waits for them, and re-layouts  8.76 us (3%)
    psum x1, waiting for transfers between devices, per_device(): recon = lax.psum(partial_value, LATENT) + dec_bias[0]  140 us
    all_to_all x1, blocking collectives, sent_to_all(): lax.all_to_all(jnp.broadcast_to(x[None], (count, *x.shape)), axis, 0, 0,...  41.2 us
    psum x4, blocking collectives, over_axes(): x = lax.psum(x, axis)  32.5 us
    psum x1, waiting for transfers between devices, per_device(): preact, norm_sum = lax.psum((layer_pre, row_norm), 'layer')  17.8 us
    unnamed x13, local copies, waits for them, and re-layouts  7.77 us
    dot_general x1, matrix products, per_device(): jnp.einsum('td,tf->df', token_all, preact_grad, preferred_element_type=jn...  6.68 us
    dot_general x1, matrix products, per_device(): jnp.einsum('tf,td->fd', code_b, error_b, preferred_element_type=jnp.float32)  6.65 us
  transfers between devices with their start and end apart: 3, of which 2 were waited for; matrix products, arithmetic and copies ran while one was open for 3% of the time, Pallas kernels for 0%

commit v1 on v0

--- a/solution.py
+++ b/solution.py
@@ -7,6 +7,11 @@
 LATENT = ("latent_0", "latent_1", "latent_2")
 LAYER_LATENT = ("layer", "latent_0", "latent_1", "latent_2")
 sparsity_weight = 0.4
+
+
+def axis_by_axis(array, one, other):
+    inner = lax.psum(array, one)
+    return lax.psum(inner, other)
 
 
 def sent_to_all(x, axis):
@@ -47,7 +52,7 @@
     layer_index = lax.axis_index("layer")
     latent_index = lax.axis_index(LATENT)
     partial_value = jnp.dot(code_b, decoder, preferred_element_type=jnp.float32)
-    recon = lax.psum(partial_value, LATENT) + dec_bias[0]
+    recon = axis_by_axis(partial_value, ("latent_1", "latent_2"), "latent_0") + dec_bias[0]
     error_full = recon - token_all.astype(jnp.float32)
     error_b = error_full.astype(jnp.bfloat16)
     square_part = jnp.where(latent_index == 0, 0.5 * jnp.sum(error_full * error_full), 0.0)

time: 296 us -> 358 us (1.21)
  waiting for transfers between devices: 158 us -> 218 us
    psum x1 -> x2, waiting for transfers between devices: 140 us -> 200 us  [the longest x1 105 us: axis_by_axis(): inner = lax.psum(array, one)]
  transfers between devices with their start and end apart: 3 -> 4, of which waited for: 2 -> 3; matrix products, arithmetic and copies ran while one was open for 3% -> 3% of each run, Pallas kernels for 0% -> 0%
where the time goes in v1:
time: 358 us
  waiting for transfers between devices  218 us (61%)
  blocking collectives  78.3 us (22%)
  matrix products  25.1 us (7%)
  between operations  16.9 us (5%)
  other arithmetic  10.7 us (3%)
  local copies, waits for them, and re-layouts  8.76 us (2%)
    psum x1, waiting for transfers between devices, axis_by_axis(): inner = lax.psum(array, one)  105 us
    psum x1, waiting for transfers between devices, axis_by_axis(): return lax.psum(inner, other)  94.9 us
    all_to_all x1, blocking collectives, sent_to_all(): lax.all_to_all(jnp.broadcast_to(x[None], (count, *x.shape)), axis, 0, 0,...  41.2 us
    psum x4, blocking collectives, over_axes(): x = lax.psum(x, axis)  34.6 us
    psum x1, waiting for transfers between devices, per_device(): preact, norm_sum = lax.psum((layer_pre, row_norm), 'layer')  17.8 us
    unnamed x13, local copies, waits for them, and re-layouts  7.77 us
  transfers between devices with their start and end apart: 4, of which 3 were waited for; matrix products, arithmetic and copies ran while one was open for 3% of the time, Pallas kernels for 0%

profile of v1, /device:TPU:0, one launch (start us, length us, event | category | flops | bytes accessed | tf_op | source)
XLA Modules:
  0.0 357.7 jit_solution(16903480778219382350)
XLA Ops:
  7.2 0.0 all-reduce.5.cloned.1.call-start
  7.2 1.0 broadcast_in_dim.9
  8.2 0.0 copy-start.5
  8.2 41.2 %all_to_all.5 = bf16[64,8,2048]{2,1,0:T(8,128)(2,1)S(1)} all-to-all(bf16[64,8,2048]{2,1,0:T(8,128)(2,1)S(1)} %broadcast_in_dim.9), channel_id=1, replica_groups=mesh['layer'=2,'latent_0'=4,'latent_1'=4,'latent_2'=4] {'latent_0','late..., dimensions={0} | all-to-all | bytes 4194304 | tf_op jit(solution)/shard_map/all_to_all | solution.py:19
  49.4 0.0 copy-done.5
  49.4 3.7 %fusion.8 = f32[512,1024]{1,0:T(8,128)} fusion(bf16[1,2048,1024]{2,1,0:T(8,128)(2,1)S(1)} %copy-done.5, bf16[64,8,2048]{2,1,0:T(8,128)(2,1)S(1)} %all_to_all.5), kind=kOutput, calls=%fused_computation.10 | convolution fusion | flops 2147483648 | bytes 8388608 | tf_op jit(solution)/shard_map/dot_general | solution.py:44
  53.1 0.0 all-reduce.5.cloned.1.call-update
  53.1 0.0 copy-start.4
  53.1 0.0 all-reduce.7.cloned.1.call-start
  53.2 3.1 fusion
  56.3 2.5 psum.67
  58.8 17.8 %all-reduce.5.cloned.1.call-done = f32[512,1024]{1,0:T(8,128)} async-done(((f32[512,1024]{1,0:T(8,128)}), f32[512,1024]{1,0:T(8,128)}) %all-reduce.5.cloned.1.call-update) | async-done | bytes 2097168 | tf_op jit(solution)/shard_map/psum | solution.py:47
  76.5 3.6 %multiply_reduce_fusion.1 = (f32[]{:T(128)}, f32[1024]{0:T(1024)S(1)}, bf16[512,1024]{1,0:T(8,128)(2,1)S(1)}) fusion(f32[1024]{0:T(1024)S(1)} %psum.67, s32[512,1024]{1,0:T(8,128)} %param.11, f32[512,1024]{1,0:T(8,128)} %all-reduce.5.cloned.1.call-done, f32[1024]{0:T(1024)S(1)} %copy-done.4), kind=kLoop, calls=%fused_computation.19 | loop fusion | flops 3668991 | bytes 5255172 | tf_op jit(solution)/shard_map/reduce_sum | solution.py:71
  80.1 4.4 %fusion.6 = f32[512,2048]{1,0:T(8,128)} fusion(bf16[1,1024,2048]{2,1,0:T(8,128)(2,1)S(1)} %copy-done, bf16[512,1024]{1,0:T(8,128)(2,1)S(1)} %get-tuple-element.8), kind=kOutput, calls=%fused_computation.8 | convolution fusion | flops 2147483648 | bytes 9437184 | tf_op jit(solution)/shard_map/dot_general | solution.py:54
  84.5 0.0 all-reduce.7.cloned.1.call-update
  84.5 0.0 all-reduce.9.cloned.1.call-start
  84.6 105.1 %all-reduce.7.cloned.1.call-done = f32[512,2048]{1,0:T(8,128)} async-done(((f32[512,2048]{1,0:T(8,128)}), f32[512,2048]{1,0:T(8,128)}) %all-reduce.7.cloned.1.call-update) | async-done | bytes 4194320 | tf_op jit(solution)/shard_map/psum | solution.py:13
  189.7 0.0 all-reduce.9.cloned.1.call-update
  189.7 0.0 all-reduce.11.cloned.1.call-start
  189.7 94.9 %all-reduce.9.cloned.1.call-done = f32[512,2048]{1,0:T(8,128)} async-done(((f32[512,2048]{1,0:T(8,128)}), f32[512,2048]{1,0:T(8,128)}) %all-reduce.9.cloned.1.call-update) | async-done | bytes 4194320 | tf_op jit(solution)/shard_map/psum | solution.py:14
  284.6 0.0 copy-done.3
  284.6 4.0 %multiply_reduce_fusion = (f32[]{:T(128)}, bf16[512,2048]{1,0:T(8,128)(2,1)S(1)}) fusion(f32[512,2048]{1,0:T(8,128)} %all-reduce.9.cloned.1.call-done, bf16[64,8,2048]{2,1,0:T(8,128)(2,1)S(1)} %all_to_all.5, f32[2048]{0:T(1024)S(1)} %bitcast.32), kind=kLoop, calls=%fused_computation.12 | loop fusion | flops 6291455 | bytes 8396804 | tf_op jit(solution)/shard_map/reduce_sum | solution.py:58
  288.7 1.3 copy-done.2
  290.0 3.7 %fusion.4 = f32[512,1024]{1,0:T(8,128)} fusion(bf16[512,2048]{1,0:T(8,128)(2,1)S(1)} %get-tuple-element.10, bf16[1,1024,2048]{2,1,0:T(8,128)(2,1)S(1)} %copy-done.1), kind=kOutput, calls=%fused_computation.6 | convolution fusion | flops 2147483648 | bytes 8388608 | tf_op jit(solution)/shard_map/td,fd->tf/dot_general | solution.py:59
  293.7 0.0 all-reduce.11.cloned.1.call-update
  295.0 3.0 psum.68
  298.0 9.2 %psum.69 = f32[]{:T(128)} all-reduce(f32[]{:T(128)} %psum.68), channel_id=1, replica_groups=mesh['layer'=2,'latent_0'=4,'latent_1'=4,'latent_2'=4] {'latent_0'}, use_global_device_ids=true, to_apply=%region_10.11 | all-reduce | flops 1 | bytes 8 | tf_op jit(solution)/shard_map/psum | solution.py:35
  307.2 11.0 %psum.70 = f32[]{:T(128)} all-reduce(f32[]{:T(128)} %psum.69), channel_id=1, replica_groups=mesh['layer'=2,'latent_0'=4,'latent_1'=4,'latent_2'=4] {'latent_1'}, use_global_device_ids=true, to_apply=%region_11.12 | all-reduce | flops 1 | bytes 8 | tf_op jit(solution)/shard_map/psum | solution.py:35
  318.2 11.5 %psum.71 = f32[]{:T(128)} all-reduce(f32[]{:T(128)} %psum.70), channel_id=1, replica_groups=mesh['layer'=2,'latent_0'=4,'latent_1'=4,'latent_2'=4] {'latent_2'}, use_global_device_ids=true, to_apply=%region_12.13 | all-reduce | flops 1 | bytes 8 | tf_op jit(solution)/shard_map/psum | solution.py:35
  330.3 6.6 %fusion.10 = bf16[1,1024,2048]{2,1,0:T(8,128)(2,1)} fusion(f32[1024]{0:T(1024)S(1)} %add_sqrt_fusion, bf16[1,1024,2048]{2,1,0:T(8,128)(2,1)} %param.9, f32[1024]{0:T(1024)S(1)} %broadcast_multiply_fusion, bf16[512,2048]{1,0:T(8,128)(2,1)} %copy-done.2, bf16[512,1024]{1,0:T(8,128)(2,1)S(1)} %get-tuple-element.8), kind=kOutput, calls=%fused_computation.15 | convolution fusion | flops 2157969408 | bytes 11542528 | tf_op jit(solution)/shard_map/tf,td->fd/dot_general | solution.py:68
  337.0 6.7 %convert_bitcast_fusion = bf16[1,2048,1024]{1,2,0:T(8,128)(2,1)} fusion(bf16[64,8,2048]{2,1,0:T(8,128)(2,1)S(1)} %all_to_all.5, f32[512,1024]{1,0:T(8,128)} %all-reduce.11.cloned.1.call-done, s32[512,1024]{1,0:T(8,128)} %param.11, f32[1024]{0:T(1024)S(1)} %broadcast_multiply_fusion.1), kind=kOutput, calls=%fused_computation.13 | convolution fusion | flops 2151677952 | bytes 10489856 | tf_op jit(solution)/shard_map/td,tf->df/dot_general | solution.py:62
  343.7 6.4 %copy.9 = bf16[1,2048,1024]{2,1,0:T(8,128)(2,1)} copy(bf16[1,2048,1024]{1,2,0:T(8,128)(2,1)} %convert_bitcast_fusion) | data formatting | bytes 8388608
  (11 shorter events, 0.0 us)
Async XLA Ops:
  7.2 69.4 %all-reduce.5.cloned.1.call-start = ((), (), s32[]{:S(2)}) async-start(), calls=%async_computation.1 | async-start | bytes 4194304 | tf_op jit(solution)/shard_map/psum | solution.py:47
  8.2 41.2 %copy-start.5 = (bf16[1,2048,1024]{2,1,0:T(8,128)(2,1)S(1)}, bf16[1,2048,1024]{2,1,0:T(8,128)(2,1)}, u32[]{:S(2)}) copy-start(bf16[1,2048,1024]{2,1,0:T(8,128)(2,1)} %param.7) | copy-start | bytes 12582916
  53.1 23.4 %copy-start.4 = (f32[1024]{0:T(1024)S(1)}, f32[1024]{0:T(1024)}, u32[]{:S(2)}) copy-start(f32[1024]{0:T(1024)} %param.8) | copy-start | bytes 12292
  53.1 136.5 %all-reduce.7.cloned.1.call-start = ((), (), s32[]{:S(2)}) async-start(), calls=%async_computation.2 | async-start | bytes 8388608 | tf_op jit(solution)/shard_map/psum | solution.py:13
  76.5 3.6 %copy-start = (bf16[1,1024,2048]{2,1,0:T(8,128)(2,1)S(1)}, bf16[1,1024,2048]{2,1,0:T(8,128)(2,1)}, u32[]{:S(2)}) copy-start(bf16[1,1024,2048]{2,1,0:T(8,128)(2,1)} %param.9) | copy-start | bytes 12582916
  84.5 200.1 %all-reduce.9.cloned.1.call-start = ((), (), s32[]{:S(2)}) async-start(), calls=%async_computation.3 | async-start | bytes 8388608 | tf_op jit(solution)/shard_map/psum | solution.py:14
  189.6 95.0 %copy-start.3 = (f32[1,2048]{1,0:T(1,128)S(1)}, f32[1,2048]{1,0:T(1,128)}, u32[]{:S(2)}) copy-start(f32[1,2048]{1,0:T(1,128)} %param.10) | copy-start | bytes 24580
  189.7 147.3 %all-reduce.11.cloned.1.call-start = ((), (), s32[]{:S(2)}) async-start(), calls=%async_computation.4 | async-start | bytes 4194304 | tf_op jit(solution)/shard_map/psum | solution.py:60
  284.6 5.4 %copy-start.1 = (bf16[1,1024,2048]{2,1,0:T(8,128)(2,1)S(1)}, bf16[1,1024,2048]{2,1,0:T(8,128)(2,1)}, u32[]{:S(2)}) copy-start(bf16[1,1024,2048]{2,1,0:T(8,128)(2,1)} %param.9) | copy-start | bytes 12582916
  288.7 1.4 copy-start.2
Sparse Core Ops, SparseCore 0:
  53.3 23.2 all-reduce.4
  84.7 104.9 all-reduce.6
  192.1 92.4 all-reduce.8
  293.9 26.5 all-reduce.10
